TPU v7x, 256 devices: a whole 4x4x8 slice. The times are simulated.
256 devices in a mesh: req: 32 (over y, x, core), head: 8 (over z).
Axes of the slice: x: 4, y: 4, z: 8, core: 2. Of those that a mesh axis runs over, the one named last changes fastest.
Arguments:
- queries: bfloat16 [1024, 16384], P(('req', 'head')), may hold values from -15 to 15
- cache_keys: bfloat16 [8, 32768, 1024], P(None, 'req', 'head'), may hold values from -6 to 6
- cache_values: bfloat16 [8, 32768, 1024], P(None, 'req', 'head'), may hold values from -6 to 6
- tree_keys: bfloat16 [1024, 1024], P('req', 'head'), may hold values from -10 to 10
- tree_values: bfloat16 [1024, 1024], P('req', 'head'), may hold values from -6 to 6
- parents: int32 [8, 128], replicated, may hold values from -1 to 126, as said below
- tree_sizes: int32 [8], replicated, may hold values from 16 to 128
- cache_lens: int32 [8], replicated, may hold values from 2 to 32768
Outputs:
- attended: bfloat16 [1024, 16384], P('req', 'head')
Inputs may be any that keep to these rules, and one draw needn't show every extreme that they name: parents[a, 0] = -1 (the root); for node i >= 1, parents[a, i] is a node of 0 to i - 1.
All inputs are finite; a program needn't handle non-finite values.
Results may differ from a plain program's by a relative error of at most 0.003.
Values may be sent and summed in bfloat16 or wider, within the bound.
A program may use at most 128 MiB of HBM per device.

v0:
```python
import math
import jax
import jax.numpy as jnp
from jax import lax
from jax.sharding import Mesh
from jax.sharding import PartitionSpec as P

NH = 128
KVH = 8
HD = 128
negative_fill = -1e30


def ancestry(parents):
    node_count = parents.shape[1]
    node_ids = jnp.arange(node_count, dtype=jnp.int32)
    linked = jnp.logical_or(
        parents[:, :, None] == node_ids[None, None, :], node_ids[:, None] == node_ids[None, :]
    )
    reached = linked.astype(jnp.bfloat16)
    for doubling in range((node_count - 1).bit_length()):
        squared = jnp.einsum("aij,ajk->aik", reached, reached, preferred_element_type=jnp.float32)
        reached = jnp.minimum(squared, 1.0).astype(jnp.bfloat16)
    return reached


def body(
    queries, cache_keys, cache_values, tree_keys, tree_values, parents, tree_sizes, cache_lens
):
    group_size = NH // KVH
    softmax_scale = 1.0 / math.sqrt(HD)
    request = lax.axis_index("rh")
    quarter = lax.axis_index("rl")
    n_lo = lax.axis_size("rl")
    n_hi = lax.axis_size("rh")
    cache_block = cache_keys.shape[1]
    kv_local = cache_keys.shape[2] // HD
    heads_local = kv_local * group_size
    node_count = parents.shape[1]
    rows_owned = tree_keys.shape[0]
    by_head = lax.all_to_all(queries, "head", split_axis=1, concat_axis=0, tiled=True)
    query_block = lax.all_gather(by_head, "rl", axis=0, tiled=True)
    query_block = query_block.reshape(node_count, kv_local, group_size, HD)
    both = jnp.concatenate([cache_keys, cache_values], axis=2)
    mine = lax.all_to_all(both, "rh", split_axis=0, concat_axis=1, tiled=True)[0]
    mine = mine.reshape(n_hi, cache_block, 2, kv_local, HD)
    reached = ancestry(parents)
    ancestors = lax.dynamic_index_in_dim(reached, request, 0, keepdims=False)
    ancestors = lax.dynamic_slice_in_dim(ancestors, quarter * rows_owned, rows_owned, 1)
    live_tree_all = ancestors > 0.5
    length = lax.dynamic_index_in_dim(cache_lens, request, 0, keepdims=False)
    local_tree_keys = tree_keys.reshape(rows_owned, kv_local, HD)
    local_tree_values = tree_values.reshape(rows_owned, kv_local, HD)

    def one_group(s):
        block = s * n_lo + quarter
        positions = block * cache_block + jnp.arange(cache_block, dtype=jnp.int32)
        live_cache = positions < length
        live_tree = jnp.logical_and(live_tree_all, s == request)
        block_keys = mine[s, :, 0]
        block_values = mine[s, :, 1]
        cache_scores = (
            jnp.einsum(
                "igqd,pgd->igqp", query_block, block_keys, preferred_element_type=jnp.float32
            )
            * softmax_scale
        )
        cache_scores = jnp.where(live_cache[None, None, None, :], cache_scores, negative_fill)
        tree_scores = (
            jnp.einsum(
                "igqd,rgd->igqr", query_block, local_tree_keys, preferred_element_type=jnp.float32
            )
            * softmax_scale
        )
        tree_scores = jnp.where(live_tree[:, None, None, :], tree_scores, negative_fill)
        peaks = jnp.maximum(jnp.max(cache_scores, axis=3), jnp.max(tree_scores, axis=3))
        cache_weights = jnp.where(
            live_cache[None, None, None, :], jnp.exp(cache_scores - peaks[..., None]), 0.0
        )
        tree_weights = jnp.where(
            live_tree[:, None, None, :], jnp.exp(tree_scores - peaks[..., None]), 0.0
        )
        totals = jnp.sum(cache_weights, axis=3) + jnp.sum(tree_weights, axis=3)
        group_sums = jnp.einsum(
            "igqp,pgd->igqd",
            cache_weights.astype(jnp.bfloat16),
            block_values,
            preferred_element_type=jnp.float32,
        )
        group_sums = group_sums + jnp.einsum(
            "igqr,rgd->igqd",
            tree_weights.astype(jnp.bfloat16),
            local_tree_values,
            preferred_element_type=jnp.float32,
        )
        floored = jnp.maximum(totals, 1.0)
        partial_value = group_sums / floored[..., None]
        log_total = peaks + jnp.log(floored)
        return (
            partial_value.reshape(node_count, heads_local, HD),
            log_total.reshape(node_count, heads_local),
        )

    partials, log_totals = lax.map(one_group, jnp.arange(n_hi, dtype=jnp.int32))
    top = jnp.max(log_totals, axis=0)
    weights = jnp.exp(log_totals - top)
    den = jnp.sum(weights, axis=0)
    acc = jnp.sum(weights[..., None] * partials, axis=0)
    payload = jnp.concatenate(
        [acc.reshape(node_count, heads_local * HD), den, top], axis=1
    ).reshape(n_lo, rows_owned, heads_local * HD + 2 * heads_local)
    gathered = lax.all_to_all(payload, "rl", split_axis=0, concat_axis=0, tiled=True)
    got_acc = gathered[:, :, : heads_local * HD].reshape(n_lo, rows_owned, heads_local, HD)
    got_den = gathered[:, :, heads_local * HD : heads_local * HD + heads_local]
    got_top = gathered[:, :, heads_local * HD + heads_local :]
    highest = jnp.max(got_top, axis=0)
    scale = jnp.exp(got_top - highest)
    num = jnp.sum(scale[..., None] * got_acc, axis=0)
    total = jnp.sum(scale * got_den, axis=0)
    merged = (num / total[..., None]).reshape(rows_owned, heads_local * HD)
    row_nodes = quarter * rows_owned + jnp.arange(rows_owned, dtype=jnp.int32)
    live_size = lax.dynamic_index_in_dim(tree_sizes, request, 0, keepdims=False)
    live_rows = row_nodes < live_size
    return jnp.where(live_rows[:, None], merged, 0.0).astype(jnp.bfloat16)


def solution(mesh):

    def run(
        queries, cache_keys, cache_values, tree_keys, tree_values, parents, tree_sizes, cache_lens
    ):
        n_hi = cache_keys.shape[0]
        n_lo = mesh.shape["req"] // n_hi
        split = Mesh(mesh.devices.reshape(n_hi, n_lo, mesh.shape["head"]), ("rh", "rl", "head"))
        rows = ("rh", "rl")
        placed = (
            P(("rh", "rl", "head"), None),
            P(None, rows, "head"),
            P(None, rows, "head"),
            P(rows, "head"),
            P(rows, "head"),
            P(),
            P(),
            P(),
        )
        return jax.shard_map(
            body, mesh=split, in_specs=placed, out_specs=P(rows, "head"), check_vma=False
        )(
            queries,
            cache_keys,
            cache_values,
            tree_keys,
            tree_values,
            parents,
            tree_sizes,
            cache_lens,
        )

    return run
```

profile of v0, /device:TPU:1, one launch (start us, length us, event | category | flops | bytes accessed | tf_op | source)
XLA Modules:
  0.0 273.4 jit_solution(10835699050133776124)
XLA Ops:
  0.0 9.1 %all-to-all-start.1 = ((bf16[4,8,2048]{2,0,1:T(4,128)(2,1)}), bf16[4,8,2048]{2,0,1:T(4,128)(2,1)S(1)}, u32[]{:S(2)}, u32[]{:S(2)}) async-start(bf16[4,8,2048]{2,0,1:T(4,128)(2,1)} %bitcast.168), calls=%async_computation.1 | async-start | bytes 262144 | tf_op jit(solution)/shard_map/all_to_all | solution.py:41
  9.2 2.9 %copy.62 = bf16[8,1024,128]{1,2,0:T(8,128)(2,1)S(1)} copy(bf16[8,1024,128]{2,1,0:T(8,128)(2,1)} %param.12) | data formatting | bytes 4194304 | tf_op args[2]
  12.0 3.9 %copy.61 = bf16[8,1024,128]{1,2,0:T(8,128)(2,1)} copy(bf16[8,1024,128]{2,1,0:T(8,128)(2,1)} %param.11) | data formatting | bytes 4194304 | tf_op args[1]
  16.0 4.2 %pad_maximum_fusion = bf16[8,1024,256]{1,2,0:T(8,128)(2,1)} fusion(bf16[8,1024,128]{1,2,0:T(8,128)(2,1)S(1)} %copy.62, bf16[8,1024,128]{1,2,0:T(8,128)(2,1)} %copy.61), kind=kLoop, calls=%fused_computation.47 | loop fusion | flops 8388608 | bytes 8388608 | tf_op jit(solution)/shard_map/concatenate | solution.py:44
  20.2 6.7 %all-to-all-start = ((bf16[8,1024,256]{1,2,0:T(8,128)(2,1)}), bf16[8,1024,256]{1,2,0:T(8,128)(2,1)}, u32[]{:S(2)}, u32[]{:S(2)}) async-start(bf16[8,1024,256]{1,2,0:T(8,128)(2,1)} %pad_maximum_fusion), calls=%async_computation | async-start | bytes 8388608 | tf_op jit(solution)/shard_map/all_to_all | solution.py:45
  27.5 0.9 fusion.38
  29.7 47.9 %all_gather.3 = bf16[128,2048]{1,0:T(8,128)(2,1)S(1)} all-gather(bf16[32,2048]{1,0:T(8,128)(2,1)S(1)} %all_to_all.28), channel_id=1, replica_groups=mesh['rh'=8,'rl'=4,'head'=8] {'rl'}, dimensions={0}, use_global_device_ids=true | all-gather | bytes 655360 | tf_op jit(solution)/shard_map/all_gather | solution.py:42
  78.5 6.5 %copy.69 = bf16[8,1024,2,1,128]{4,1,3,2,0:T(8,128)(2,1)} copy(bf16[8,1024,2,1,128]{1,4,2,0,3:T(8,128)(2,1)} %bitcast.20) | data formatting | bytes 8388608 | tf_op jit(solution)/shard_map/while | solution.py:104
  85.0 160.4 %while.14 = (s32[]{:T(128)}, f32[8,128,16,128]{1,3,2,0:T(8,128)}, f32[8,128,16]{1,2,0:T(8,128)S(1)}, s32[8]{0:T(128)S(1)}, bf16[8,1024,2,1,128]{4,1,3,2,0:T(8,12...) while((s32[]{:T(128)}, f32[8,128,16,128]{1,3,2,0:T(8,128)}, ...), condition=%wide.region_5.6_spmd, body=%wide.region_0.5_spmd.sunk | while | flops 1119164416 | bytes 55485768 | solution.py:104
  85.0 0.7 dynamic_slice.52
  88.9 5.5 %bitcast_reduce_fusion.2 = (f32[128,16]{0,1:T(8,128)S(1)}, f32[1024,128,16]{1,0,2:T(8,128)}) fusion(pred[1024]{0:T(1024)(128)(4,1)S(1)} %add_compare_fusion.3, bf16[128,1,16,128]{3,0,2,1:T(8,128)(2,1)S(1)} %get-tuple-element.349, bf16[8,1024,2,1,128]{4,1,3,2,0:T(8,128)(2,1)} %get-tuple-element.346, s32[]{:T(128)S(6)} %select_n.118), kind=kOutput, calls=%fused_computation.1.clone.1 | convolution fusion | flops 543160320 | bytes 9184260 | tf_op jit(solution)/shard_map/while/body/eval_jaxpr/igqd,pgd->igqp/dot_general | solution.py:63
  95.2 5.8 %fusion.85 = f32[128,128,16]{1,0,2:T(8,128)S(1)} fusion(f32[1024,128,16]{1,0,2:T(8,128)} %get-tuple-element.304, f32[128,16]{0,1:T(8,128)S(1)} %max.47, pred[1024]{0:T(1024)(128)(4,1)S(1)} %add_compare_fusion.3, bf16[8,1024,2,1,128]{4,1,3,2,0:T(8,128)(2,1)} %get-tuple-element.346, s32[]{:T(128)S(6)} %select_n.118), kind=kOutput, calls=%fused_computation.8.clone.1 | convolution fusion | flops 547356672 | bytes 9709572 | tf_op jit(solution)/shard_map/while/body/eval_jaxpr/igqp,pgd->igqd/dot_general | solution.py:84
  101.0 2.5 fusion.86
  103.7 1.3 bitcast_dynamic-update-slice_fusion.5
  105.0 0.7 dynamic_slice.52
  108.9 5.5 %bitcast_reduce_fusion.2 = (f32[128,16]{0,1:T(8,128)S(1)}, f32[1024,128,16]{1,0,2:T(8,128)}) fusion(pred[1024]{0:T(1024)(128)(4,1)S(1)} %add_compare_fusion.3, bf16[128,1,16,128]{3,0,2,1:T(8,128)(2,1)S(1)} %get-tuple-element.349, bf16[8,1024,2,1,128]{4,1,3,2,0:T(8,128)(2,1)} %get-tuple-element.346, s32[]{:T(128)S(6)} %select_n.118), kind=kOutput, calls=%fused_computation.1.clone.1 | convolution fusion | flops 543160320 | bytes 9184260 | tf_op jit(solution)/shard_map/while/body/eval_jaxpr/igqd,pgd->igqp/dot_general | solution.py:63
  115.2 5.8 %fusion.85 = f32[128,128,16]{1,0,2:T(8,128)S(1)} fusion(f32[1024,128,16]{1,0,2:T(8,128)} %get-tuple-element.304, f32[128,16]{0,1:T(8,128)S(1)} %max.47, pred[1024]{0:T(1024)(128)(4,1)S(1)} %add_compare_fusion.3, bf16[8,1024,2,1,128]{4,1,3,2,0:T(8,128)(2,1)} %get-tuple-element.346, s32[]{:T(128)S(6)} %select_n.118), kind=kOutput, calls=%fused_computation.8.clone.1 | convolution fusion | flops 547356672 | bytes 9709572 | tf_op jit(solution)/shard_map/while/body/eval_jaxpr/igqp,pgd->igqd/dot_general | solution.py:84
  121.1 2.5 fusion.86
  123.7 1.4 bitcast_dynamic-update-slice_fusion.5
  129.0 5.5 %bitcast_reduce_fusion.2 = (f32[128,16]{0,1:T(8,128)S(1)}, f32[1024,128,16]{1,0,2:T(8,128)}) fusion(pred[1024]{0:T(1024)(128)(4,1)S(1)} %add_compare_fusion.3, bf16[128,1,16,128]{3,0,2,1:T(8,128)(2,1)S(1)} %get-tuple-element.349, bf16[8,1024,2,1,128]{4,1,3,2,0:T(8,128)(2,1)} %get-tuple-element.346, s32[]{:T(128)S(6)} %select_n.118), kind=kOutput, calls=%fused_computation.1.clone.1 | convolution fusion | flops 543160320 | bytes 9184260 | tf_op jit(solution)/shard_map/while/body/eval_jaxpr/igqd,pgd->igqp/dot_general | solution.py:63
  135.3 5.8 %fusion.85 = f32[128,128,16]{1,0,2:T(8,128)S(1)} fusion(f32[1024,128,16]{1,0,2:T(8,128)} %get-tuple-element.304, f32[128,16]{0,1:T(8,128)S(1)} %max.47, pred[1024]{0:T(1024)(128)(4,1)S(1)} %add_compare_fusion.3, bf16[8,1024,2,1,128]{4,1,3,2,0:T(8,128)(2,1)} %get-tuple-element.346, s32[]{:T(128)S(6)} %select_n.118), kind=kOutput, calls=%fused_computation.8.clone.1 | convolution fusion | flops 547356672 | bytes 9709572 | tf_op jit(solution)/shard_map/while/body/eval_jaxpr/igqp,pgd->igqd/dot_general | solution.py:84
  141.2 2.5 fusion.86
  143.8 1.3 bitcast_dynamic-update-slice_fusion.5
  149.1 5.5 %bitcast_reduce_fusion.2 = (f32[128,16]{0,1:T(8,128)S(1)}, f32[1024,128,16]{1,0,2:T(8,128)}) fusion(pred[1024]{0:T(1024)(128)(4,1)S(1)} %add_compare_fusion.3, bf16[128,1,16,128]{3,0,2,1:T(8,128)(2,1)S(1)} %get-tuple-element.349, bf16[8,1024,2,1,128]{4,1,3,2,0:T(8,128)(2,1)} %get-tuple-element.346, s32[]{:T(128)S(6)} %select_n.118), kind=kOutput, calls=%fused_computation.1.clone.1 | convolution fusion | flops 543160320 | bytes 9184260 | tf_op jit(solution)/shard_map/while/body/eval_jaxpr/igqd,pgd->igqp/dot_general | solution.py:63
  155.3 5.8 %fusion.85 = f32[128,128,16]{1,0,2:T(8,128)S(1)} fusion(f32[1024,128,16]{1,0,2:T(8,128)} %get-tuple-element.304, f32[128,16]{0,1:T(8,128)S(1)} %max.47, pred[1024]{0:T(1024)(128)(4,1)S(1)} %add_compare_fusion.3, bf16[8,1024,2,1,128]{4,1,3,2,0:T(8,128)(2,1)} %get-tuple-element.346, s32[]{:T(128)S(6)} %select_n.118), kind=kOutput, calls=%fused_computation.8.clone.1 | convolution fusion | flops 547356672 | bytes 9709572 | tf_op jit(solution)/shard_map/while/body/eval_jaxpr/igqp,pgd->igqd/dot_general | solution.py:84
  161.2 2.5 fusion.86
  163.8 1.3 bitcast_dynamic-update-slice_fusion.5
  169.1 5.5 %bitcast_reduce_fusion.2 = (f32[128,16]{0,1:T(8,128)S(1)}, f32[1024,128,16]{1,0,2:T(8,128)}) fusion(pred[1024]{0:T(1024)(128)(4,1)S(1)} %add_compare_fusion.3, bf16[128,1,16,128]{3,0,2,1:T(8,128)(2,1)S(1)} %get-tuple-element.349, bf16[8,1024,2,1,128]{4,1,3,2,0:T(8,128)(2,1)} %get-tuple-element.346, s32[]{:T(128)S(6)} %select_n.118), kind=kOutput, calls=%fused_computation.1.clone.1 | convolution fusion | flops 543160320 | bytes 9184260 | tf_op jit(solution)/shard_map/while/body/eval_jaxpr/igqd,pgd->igqp/dot_general | solution.py:63
  175.4 5.8 %fusion.85 = f32[128,128,16]{1,0,2:T(8,128)S(1)} fusion(f32[1024,128,16]{1,0,2:T(8,128)} %get-tuple-element.304, f32[128,16]{0,1:T(8,128)S(1)} %max.47, pred[1024]{0:T(1024)(128)(4,1)S(1)} %add_compare_fusion.3, bf16[8,1024,2,1,128]{4,1,3,2,0:T(8,128)(2,1)} %get-tuple-element.346, s32[]{:T(128)S(6)} %select_n.118), kind=kOutput, calls=%fused_computation.8.clone.1 | convolution fusion | flops 547356672 | bytes 9709572 | tf_op jit(solution)/shard_map/while/body/eval_jaxpr/igqp,pgd->igqd/dot_general | solution.py:84
  181.2 2.5 fusion.86
  183.9 1.3 bitcast_dynamic-update-slice_fusion.5
  189.1 5.5 %bitcast_reduce_fusion.2 = (f32[128,16]{0,1:T(8,128)S(1)}, f32[1024,128,16]{1,0,2:T(8,128)}) fusion(pred[1024]{0:T(1024)(128)(4,1)S(1)} %add_compare_fusion.3, bf16[128,1,16,128]{3,0,2,1:T(8,128)(2,1)S(1)} %get-tuple-element.349, bf16[8,1024,2,1,128]{4,1,3,2,0:T(8,128)(2,1)} %get-tuple-element.346, s32[]{:T(128)S(6)} %select_n.118), kind=kOutput, calls=%fused_computation.1.clone.1 | convolution fusion | flops 543160320 | bytes 9184260 | tf_op jit(solution)/shard_map/while/body/eval_jaxpr/igqd,pgd->igqp/dot_general | solution.py:63
  195.4 5.8 %fusion.85 = f32[128,128,16]{1,0,2:T(8,128)S(1)} fusion(f32[1024,128,16]{1,0,2:T(8,128)} %get-tuple-element.304, f32[128,16]{0,1:T(8,128)S(1)} %max.47, pred[1024]{0:T(1024)(128)(4,1)S(1)} %add_compare_fusion.3, bf16[8,1024,2,1,128]{4,1,3,2,0:T(8,128)(2,1)} %get-tuple-element.346, s32[]{:T(128)S(6)} %select_n.118), kind=kOutput, calls=%fused_computation.8.clone.1 | convolution fusion | flops 547356672 | bytes 9709572 | tf_op jit(solution)/shard_map/while/body/eval_jaxpr/igqp,pgd->igqd/dot_general | solution.py:84
  201.3 2.5 fusion.86
  203.9 1.4 bitcast_dynamic-update-slice_fusion.5
  209.2 5.5 %bitcast_reduce_fusion.2 = (f32[128,16]{0,1:T(8,128)S(1)}, f32[1024,128,16]{1,0,2:T(8,128)}) fusion(pred[1024]{0:T(1024)(128)(4,1)S(1)} %add_compare_fusion.3, bf16[128,1,16,128]{3,0,2,1:T(8,128)(2,1)S(1)} %get-tuple-element.349, bf16[8,1024,2,1,128]{4,1,3,2,0:T(8,128)(2,1)} %get-tuple-element.346, s32[]{:T(128)S(6)} %select_n.118), kind=kOutput, calls=%fused_computation.1.clone.1 | convolution fusion | flops 543160320 | bytes 9184260 | tf_op jit(solution)/shard_map/while/body/eval_jaxpr/igqd,pgd->igqp/dot_general | solution.py:63
  215.5 5.8 %fusion.85 = f32[128,128,16]{1,0,2:T(8,128)S(1)} fusion(f32[1024,128,16]{1,0,2:T(8,128)} %get-tuple-element.304, f32[128,16]{0,1:T(8,128)S(1)} %max.47, pred[1024]{0:T(1024)(128)(4,1)S(1)} %add_compare_fusion.3, bf16[8,1024,2,1,128]{4,1,3,2,0:T(8,128)(2,1)} %get-tuple-element.346, s32[]{:T(128)S(6)} %select_n.118), kind=kOutput, calls=%fused_computation.8.clone.1 | convolution fusion | flops 547356672 | bytes 9709572 | tf_op jit(solution)/shard_map/while/body/eval_jaxpr/igqp,pgd->igqd/dot_general | solution.py:84
  221.3 2.5 fusion.86
  224.0 1.4 bitcast_dynamic-update-slice_fusion.5
  229.3 5.5 %bitcast_reduce_fusion.2 = (f32[128,16]{0,1:T(8,128)S(1)}, f32[1024,128,16]{1,0,2:T(8,128)}) fusion(pred[1024]{0:T(1024)(128)(4,1)S(1)} %add_compare_fusion.3, bf16[128,1,16,128]{3,0,2,1:T(8,128)(2,1)S(1)} %get-tuple-element.349, bf16[8,1024,2,1,128]{4,1,3,2,0:T(8,128)(2,1)} %get-tuple-element.346, s32[]{:T(128)S(6)} %select_n.118), kind=kOutput, calls=%fused_computation.1.clone.1 | convolution fusion | flops 543160320 | bytes 9184260 | tf_op jit(solution)/shard_map/while/body/eval_jaxpr/igqd,pgd->igqp/dot_general | solution.py:63
  235.5 5.8 %fusion.85 = f32[128,128,16]{1,0,2:T(8,128)S(1)} fusion(f32[1024,128,16]{1,0,2:T(8,128)} %get-tuple-element.304, f32[128,16]{0,1:T(8,128)S(1)} %max.47, pred[1024]{0:T(1024)(128)(4,1)S(1)} %add_compare_fusion.3, bf16[8,1024,2,1,128]{4,1,3,2,0:T(8,128)(2,1)} %get-tuple-element.346, s32[]{:T(128)S(6)} %select_n.118), kind=kOutput, calls=%fused_computation.8.clone.1 | convolution fusion | flops 547356672 | bytes 9709572 | tf_op jit(solution)/shard_map/while/body/eval_jaxpr/igqp,pgd->igqd/dot_general | solution.py:84
  241.4 2.5 fusion.86
  244.0 1.3 bitcast_dynamic-update-slice_fusion.5
  245.5 4.8 %multiply_reduce_fusion = f32[128,16,128]{0,2,1:T(8,128)S(1)} fusion(f32[8,128,16,128]{1,3,2,0:T(8,128)} %get-tuple-element.146, f32[8,128,16]{1,2,0:T(8,128)S(1)} %get-tuple-element.224), kind=kLoop, calls=%fused_computation.46 | loop fusion | flops 3932160 | bytes 9502720 | tf_op jit(solution)/shard_map/reduce_sum | solution.py:108
  251.1 1.2 concatenate.17
  252.2 5.2 %all-to-all-start.2 = ((f32[4,32,2080]{2,1,0:T(8,128)}), f32[4,32,2080]{2,1,0:T(8,128)S(1)}, u32[]{:S(2)}, u32[]{:S(2)}) async-start(f32[4,32,2080]{2,1,0:T(8,128)} %concatenate.17), calls=%async_computation.2 | async-start | bytes 2228224 | tf_op jit(solution)/shard_map/all_to_all | solution.py:112
  258.7 13.1 %all-to-all-done.2 = f32[4,32,2080]{2,1,0:T(8,128)S(1)} async-done(((f32[4,32,2080]{2,1,0:T(8,128)}), f32[4,32,2080]{2,1,0:T(8,128)S(1)}, u32[]{:S(2)}, u32[]{:S(2)}) %all-to-all-start.2) | async-done | bytes 1064992 | tf_op jit(solution)/shard_map/all_to_all | solution.py:112
  272.6 0.8 fusion.48
  (134 shorter events, 16.0 us)
Async XLA Ops:
  0.0 78.3 %copy-start = (bf16[32,128]{1,0:T(8,128)(2,1)S(1)}, bf16[32,128]{1,0:T(8,128)(2,1)}, u32[]{:S(2)}) copy-start(bf16[32,128]{1,0:T(8,128)(2,1)} %param.13) | copy-start | bytes 24580
  0.0 20.2 %all-to-all-start.1 = ((bf16[4,8,2048]{2,0,1:T(4,128)(2,1)}), bf16[4,8,2048]{2,0,1:T(4,128)(2,1)S(1)}, u32[]{:S(2)}, u32[]{:S(2)}) async-start(bf16[4,8,2048]{2,0,1:T(4,128)(2,1)} %bitcast.168), calls=%async_computation.1 | async-start | bytes 262144 | tf_op jit(solution)/shard_map/all_to_all | solution.py:41
  16.0 10.9 %copy-start.3 = (s32[8]{0:T(128)S(1)}, s32[8]{0:T(128)}, u32[]{:S(2)}) copy-start(s32[8]{0:T(128)} %param.17) | copy-start | bytes 100
  16.0 11.5 %copy-start.2 = (s32[8,128]{1,0:T(8,128)S(1)}, s32[8,128]{1,0:T(8,128)}, u32[]{:S(2)}) copy-start(s32[8,128]{1,0:T(8,128)} %param.15) | copy-start | bytes 12292
  20.2 58.3 %all-to-all-start = ((bf16[8,1024,256]{1,2,0:T(8,128)(2,1)}), bf16[8,1024,256]{1,2,0:T(8,128)(2,1)}, u32[]{:S(2)}, u32[]{:S(2)}) async-start(bf16[8,1024,256]{1,2,0:T(8,128)(2,1)} %pad_maximum_fusion), calls=%async_computation | async-start | bytes 8388608 | tf_op jit(solution)/shard_map/all_to_all | solution.py:45
  26.8 58.1 %copy-start.1 = (bf16[32,128]{1,0:T(8,128)(2,1)S(1)}, bf16[32,128]{1,0:T(8,128)(2,1)}, u32[]{:S(2)}) copy-start(bf16[32,128]{1,0:T(8,128)(2,1)} %param.14) | copy-start | bytes 24580
  95.1 5.9 %slice-start = ((s8[8388608]{0:T(1024)(128)(4,1)}), s8[4194304]{0:T(1024)(128)(4,1)S(1)}, s32[]{:S(2)}) async-start(s8[8388608]{0:T(1024)(128)(4,1)} %bitcast.160), calls=%async_computation.3 | async-start | bytes 8388608 | tf_op jit(solution)/shard_map/while
  95.2 5.9 %slice-start.1 = ((s8[8388608]{0:T(1024)(128)(4,1)}), s8[4194304]{0:T(1024)(128)(4,1)S(1)}, s32[]{:S(2)}) async-start(s8[8388608]{0:T(1024)(128)(4,1)} %bitcast.160), calls=%async_computation.4 | async-start | bytes 8388608 | tf_op jit(solution)/shard_map/while
  115.1 5.9 %slice-start = ((s8[8388608]{0:T(1024)(128)(4,1)}), s8[4194304]{0:T(1024)(128)(4,1)S(1)}, s32[]{:S(2)}) async-start(s8[8388608]{0:T(1024)(128)(4,1)} %bitcast.160), calls=%async_computation.3 | async-start | bytes 8388608 | tf_op jit(solution)/shard_map/while
  115.2 5.9 %slice-start.1 = ((s8[8388608]{0:T(1024)(128)(4,1)}), s8[4194304]{0:T(1024)(128)(4,1)S(1)}, s32[]{:S(2)}) async-start(s8[8388608]{0:T(1024)(128)(4,1)} %bitcast.160), calls=%async_computation.4 | async-start | bytes 8388608 | tf_op jit(solution)/shard_map/while
  135.2 5.9 %slice-start = ((s8[8388608]{0:T(1024)(128)(4,1)}), s8[4194304]{0:T(1024)(128)(4,1)S(1)}, s32[]{:S(2)}) async-start(s8[8388608]{0:T(1024)(128)(4,1)} %bitcast.160), calls=%async_computation.3 | async-start | bytes 8388608 | tf_op jit(solution)/shard_map/while
  135.3 5.9 %slice-start.1 = ((s8[8388608]{0:T(1024)(128)(4,1)}), s8[4194304]{0:T(1024)(128)(4,1)S(1)}, s32[]{:S(2)}) async-start(s8[8388608]{0:T(1024)(128)(4,1)} %bitcast.160), calls=%async_computation.4 | async-start | bytes 8388608 | tf_op jit(solution)/shard_map/while
  155.2 5.9 %slice-start = ((s8[8388608]{0:T(1024)(128)(4,1)}), s8[4194304]{0:T(1024)(128)(4,1)S(1)}, s32[]{:S(2)}) async-start(s8[8388608]{0:T(1024)(128)(4,1)} %bitcast.160), calls=%async_computation.3 | async-start | bytes 8388608 | tf_op jit(solution)/shard_map/while
  155.3 5.9 %slice-start.1 = ((s8[8388608]{0:T(1024)(128)(4,1)}), s8[4194304]{0:T(1024)(128)(4,1)S(1)}, s32[]{:S(2)}) async-start(s8[8388608]{0:T(1024)(128)(4,1)} %bitcast.160), calls=%async_computation.4 | async-start | bytes 8388608 | tf_op jit(solution)/shard_map/while
  175.3 5.9 %slice-start = ((s8[8388608]{0:T(1024)(128)(4,1)}), s8[4194304]{0:T(1024)(128)(4,1)S(1)}, s32[]{:S(2)}) async-start(s8[8388608]{0:T(1024)(128)(4,1)} %bitcast.160), calls=%async_computation.3 | async-start | bytes 8388608 | tf_op jit(solution)/shard_map/while
  175.4 5.9 %slice-start.1 = ((s8[8388608]{0:T(1024)(128)(4,1)}), s8[4194304]{0:T(1024)(128)(4,1)S(1)}, s32[]{:S(2)}) async-start(s8[8388608]{0:T(1024)(128)(4,1)} %bitcast.160), calls=%async_computation.4 | async-start | bytes 8388608 | tf_op jit(solution)/shard_map/while
  195.3 5.9 %slice-start = ((s8[8388608]{0:T(1024)(128)(4,1)}), s8[4194304]{0:T(1024)(128)(4,1)S(1)}, s32[]{:S(2)}) async-start(s8[8388608]{0:T(1024)(128)(4,1)} %bitcast.160), calls=%async_computation.3 | async-start | bytes 8388608 | tf_op jit(solution)/shard_map/while
  195.4 5.9 %slice-start.1 = ((s8[8388608]{0:T(1024)(128)(4,1)}), s8[4194304]{0:T(1024)(128)(4,1)S(1)}, s32[]{:S(2)}) async-start(s8[8388608]{0:T(1024)(128)(4,1)} %bitcast.160), calls=%async_computation.4 | async-start | bytes 8388608 | tf_op jit(solution)/shard_map/while
  215.4 5.9 %slice-start = ((s8[8388608]{0:T(1024)(128)(4,1)}), s8[4194304]{0:T(1024)(128)(4,1)S(1)}, s32[]{:S(2)}) async-start(s8[8388608]{0:T(1024)(128)(4,1)} %bitcast.160), calls=%async_computation.3 | async-start | bytes 8388608 | tf_op jit(solution)/shard_map/while
  215.5 5.9 %slice-start.1 = ((s8[8388608]{0:T(1024)(128)(4,1)}), s8[4194304]{0:T(1024)(128)(4,1)S(1)}, s32[]{:S(2)}) async-start(s8[8388608]{0:T(1024)(128)(4,1)} %bitcast.160), calls=%async_computation.4 | async-start | bytes 8388608 | tf_op jit(solution)/shard_map/while
  235.4 5.9 %slice-start = ((s8[8388608]{0:T(1024)(128)(4,1)}), s8[4194304]{0:T(1024)(128)(4,1)S(1)}, s32[]{:S(2)}) async-start(s8[8388608]{0:T(1024)(128)(4,1)} %bitcast.160), calls=%async_computation.3 | async-start | bytes 8388608 | tf_op jit(solution)/shard_map/while
  235.5 5.9 %slice-start.1 = ((s8[8388608]{0:T(1024)(128)(4,1)}), s8[4194304]{0:T(1024)(128)(4,1)S(1)}, s32[]{:S(2)}) async-start(s8[8388608]{0:T(1024)(128)(4,1)} %bitcast.160), calls=%async_computation.4 | async-start | bytes 8388608 | tf_op jit(solution)/shard_map/while
  245.5 11.9 %copy-start.4 = (s32[8]{0:T(128)S(1)}, s32[8]{0:T(128)}, u32[]{:S(2)}) copy-start(s32[8]{0:T(128)} %param.16) | copy-start | bytes 100
  252.2 19.5 %all-to-all-start.2 = ((f32[4,32,2080]{2,1,0:T(8,128)}), f32[4,32,2080]{2,1,0:T(8,128)S(1)}, u32[]{:S(2)}, u32[]{:S(2)}) async-start(f32[4,32,2080]{2,1,0:T(8,128)} %concatenate.17), calls=%async_computation.2 | async-start | bytes 2228224 | tf_op jit(solution)/shard_map/all_to_all | solution.py:112
where the time goes:
time: 275 us; the launch traced here: 273 us
  matrix products  103 us (37%)
  blocking collectives  47.9 us (17%)
  other arithmetic  36.8 us (13%)
  loops' own time  27.8 us (10%)
  local copies, waits for them, and re-layouts  23.5 us (9%)
  starting transfers between devices  21 us (8%)
  waiting for transfers between devices  13.1 us (5%)
    all_gather x1, blocking collectives, body(): query_block = lax.all_gather(by_head, 'rl', axis=0, tiled=True)  47.9 us
    dot_general x8, matrix products, one_group(): jnp.einsum('igqp,pgd->igqd', cache_weights.astype(jnp.bfloat16), block_va...  46.3 us
    dot_general x8, matrix products, one_group(): jnp.einsum('igqd,pgd->igqp', query_block, block_keys, preferred_element_t...  43.9 us
    another operation x1, loops' own time, body(): partials, log_totals = lax.map(one_group, jnp.arange(n_hi, dtype=jnp.int32))  27.8 us
    reduce_sum x16, other arithmetic, one_group(): totals = jnp.sum(cache_weights, axis=3) + jnp.sum(tree_weights, axis=3)  20.8 us
    all_to_all x1, waiting for transfers between devices, body(): lax.all_to_all(payload, 'rl', split_axis=0, concat_axis=0, tiled=True)  13.1 us
    dot_general x8, matrix products, one_group(): jnp.einsum('igqr,rgd->igqd', tree_weights.astype(jnp.bfloat16), local_tre...  10.8 us
    all_to_all x1, starting transfers between devices, body(): lax.all_to_all(queries, 'head', split_axis=1, concat_axis=0, tiled=True)  9.15 us
  transfers between devices with their start and end apart: 3, of which 1 were waited for; matrix products, arithmetic and copies ran while one was open for 6% of the time, Pallas kernels for 0%

commit v1 on v0

--- a/solution.py
+++ b/solution.py
@@ -38,7 +38,10 @@
     heads_local = kv_local * group_size
     node_count = parents.shape[1]
     rows_owned = tree_keys.shape[0]
-    by_head = lax.all_to_all(queries, "head", split_axis=1, concat_axis=0, tiled=True)
+    by_head = jnp.concatenate(
+        lax.all_to_all(jnp.stack(jnp.split(queries, lax.axis_size("head"), axis=1)), "head", 0, 0),
+        axis=0,
+    )
     query_block = lax.all_gather(by_head, "rl", axis=0, tiled=True)
     query_block = query_block.reshape(node_count, kv_local, group_size, HD)
     both = jnp.concatenate([cache_keys, cache_values], axis=2)

time: 275 us -> 286 us (1.040)
  local copies, waits for them, and re-layouts: 23.5 us -> 34.1 us
    unnamed x12 -> x19, local copies, waits for them, and re-layouts: 6.81 us -> 16.1 us
where the time goes in v1:
time: 286 us; the launch traced here: 284 us
  matrix products  103 us (36%)
  blocking collectives  47.9 us (17%)
  other arithmetic  36.8 us (13%)
  local copies, waits for them, and re-layouts  34.1 us (12%)
  loops' own time  27.8 us (10%)
  starting transfers between devices  20.8 us (7%)
  waiting for transfers between devices  13.1 us (5%)
    all_gather x1, blocking collectives, body(): query_block = lax.all_gather(by_head, 'rl', axis=0, tiled=True)  47.9 us
    dot_general x8, matrix products, one_group(): jnp.einsum('igqp,pgd->igqd', cache_weights.astype(jnp.bfloat16), block_va...  46.3 us
    dot_general x8, matrix products, one_group(): jnp.einsum('igqd,pgd->igqp', query_block, block_keys, preferred_element_t...  43.9 us
    another operation x1, loops' own time, body(): partials, log_totals = lax.map(one_group, jnp.arange(n_hi, dtype=jnp.int32))  27.8 us
    reduce_sum x16, other arithmetic, one_group(): totals = jnp.sum(cache_weights, axis=3) + jnp.sum(tree_weights, axis=3)  20.8 us
    unnamed x19, local copies, waits for them, and re-layouts  16.1 us
    all_to_all x1, waiting for transfers between devices, body(): lax.all_to_all(payload, 'rl', split_axis=0, concat_axis=0, tiled=True)  13.1 us
    dot_general x8, matrix products, one_group(): jnp.einsum('igqr,rgd->igqd', tree_weights.astype(jnp.bfloat16), local_tre...  10.8 us
  transfers between devices with their start and end apart: 3, of which 1 were waited for; matrix products, arithmetic and copies ran while one was open for 6% of the time, Pallas kernels for 0%

profile of v1, /device:TPU:1, one launch (start us, length us, event | category | flops | bytes accessed | tf_op | source)
XLA Modules:
  0.0 283.9 jit_solution(181621779907443237)
XLA Ops:
  0.0 1.3 constant_dynamic-update-slice_fusion.7
  1.3 1.3 constant_dynamic-update-slice_fusion.6
  2.7 1.3 constant_dynamic-update-slice_fusion.5
  4.0 1.3 constant_dynamic-update-slice_fusion.4
  5.3 1.3 constant_dynamic-update-slice_fusion.3
  6.7 1.3 constant_dynamic-update-slice_fusion.2
  8.0 1.3 constant_dynamic-update-slice_fusion.1
  10.6 9.0 %all-to-all-start.1 = ((bf16[8,4,2048]{2,1,0:T(4,128)(2,1)}), bf16[8,4,2048]{2,1,0:T(4,128)(2,1)S(1)}, u32[]{:S(2)}, u32[]{:S(2)}) async-start(bf16[8,4,2048]{2,1,0:T(4,128)(2,1)} %constant_dynamic-update-slice_fusion), calls=%async_computation.1 | async-start | bytes 262144 | tf_op jit(solution)/shard_map/all_to_all | solution.py:42
  19.7 2.9 %copy.72 = bf16[8,1024,128]{1,2,0:T(8,128)(2,1)S(1)} copy(bf16[8,1024,128]{2,1,0:T(8,128)(2,1)} %param.12) | data formatting | bytes 4194304 | tf_op args[2]
  22.5 3.9 %copy.71 = bf16[8,1024,128]{1,2,0:T(8,128)(2,1)} copy(bf16[8,1024,128]{2,1,0:T(8,128)(2,1)} %param.11) | data formatting | bytes 4194304 | tf_op args[1]
  26.5 4.2 %pad_maximum_fusion = bf16[8,1024,256]{1,2,0:T(8,128)(2,1)} fusion(bf16[8,1024,128]{1,2,0:T(8,128)(2,1)S(1)} %copy.72, bf16[8,1024,128]{1,2,0:T(8,128)(2,1)} %copy.71), kind=kLoop, calls=%fused_computation.47 | loop fusion | flops 8388608 | bytes 8388608 | tf_op jit(solution)/shard_map/concatenate | solution.py:47
  30.7 6.7 %all-to-all-start = ((bf16[8,1024,256]{1,2,0:T(8,128)(2,1)}), bf16[8,1024,256]{1,2,0:T(8,128)(2,1)}, u32[]{:S(2)}, u32[]{:S(2)}) async-start(bf16[8,1024,256]{1,2,0:T(8,128)(2,1)} %pad_maximum_fusion), calls=%async_computation | async-start | bytes 8388608 | tf_op jit(solution)/shard_map/all_to_all | solution.py:48
  40.3 47.9 %all_gather.3 = bf16[128,2048]{1,0:T(8,128)(2,1)S(1)} all-gather(bf16[32,2048]{1,0:T(8,128)(2,1)S(1)} %reshape.223), channel_id=1, replica_groups=mesh['rh'=8,'rl'=4,'head'=8] {'rl'}, dimensions={0}, use_global_device_ids=true | all-gather | bytes 655360 | tf_op jit(solution)/shard_map/all_gather | solution.py:45
  89.0 6.5 %copy.78 = bf16[8,1024,2,1,128]{4,1,3,2,0:T(8,128)(2,1)} copy(bf16[8,1024,2,1,128]{1,4,2,0,3:T(8,128)(2,1)} %bitcast.20) | data formatting | bytes 8388608 | tf_op jit(solution)/shard_map/while | solution.py:107
  95.5 160.4 %while.14 = (s32[]{:T(128)}, f32[8,128,16,128]{1,3,2,0:T(8,128)}, f32[8,128,16]{1,2,0:T(8,128)S(1)}, s32[8]{0:T(128)S(1)}, bf16[8,1024,2,1,128]{4,1,3,2,0:T(8,12...) while((s32[]{:T(128)}, f32[8,128,16,128]{1,3,2,0:T(8,128)}, ...), condition=%wide.region_5.6_spmd, body=%wide.region_0.5_spmd.sunk | while | flops 1119164416 | bytes 55485768 | solution.py:107
  99.4 5.5 %bitcast_reduce_fusion.2 = (f32[128,16]{0,1:T(8,128)S(1)}, f32[1024,128,16]{1,0,2:T(8,128)}) fusion(pred[1024]{0:T(1024)(128)(4,1)S(1)} %add_compare_fusion.3, bf16[128,1,16,128]{3,0,2,1:T(8,128)(2,1)S(1)} %get-tuple-element.361, bf16[8,1024,2,1,128]{4,1,3,2,0:T(8,128)(2,1)} %get-tuple-element.358, s32[]{:T(128)S(6)} %select_n.118), kind=kOutput, calls=%fused_computation.1.clone.1 | convolution fusion | flops 543160320 | bytes 9184260 | tf_op jit(solution)/shard_map/while/body/eval_jaxpr/igqd,pgd->igqp/dot_general | solution.py:66
  105.7 5.8 %fusion.84 = f32[128,128,16]{1,0,2:T(8,128)S(1)} fusion(f32[1024,128,16]{1,0,2:T(8,128)} %get-tuple-element.316, f32[128,16]{0,1:T(8,128)S(1)} %max.47, pred[1024]{0:T(1024)(128)(4,1)S(1)} %add_compare_fusion.3, bf16[8,1024,2,1,128]{4,1,3,2,0:T(8,128)(2,1)} %get-tuple-element.358, s32[]{:T(128)S(6)} %select_n.118), kind=kOutput, calls=%fused_computation.8.clone.1 | convolution fusion | flops 547356672 | bytes 9709572 | tf_op jit(solution)/shard_map/while/body/eval_jaxpr/igqp,pgd->igqd/dot_general | solution.py:87
  111.5 2.5 fusion.85
  114.2 1.3 bitcast_dynamic-update-slice_fusion.5
  119.4 5.5 %bitcast_reduce_fusion.2 = (f32[128,16]{0,1:T(8,128)S(1)}, f32[1024,128,16]{1,0,2:T(8,128)}) fusion(pred[1024]{0:T(1024)(128)(4,1)S(1)} %add_compare_fusion.3, bf16[128,1,16,128]{3,0,2,1:T(8,128)(2,1)S(1)} %get-tuple-element.361, bf16[8,1024,2,1,128]{4,1,3,2,0:T(8,128)(2,1)} %get-tuple-element.358, s32[]{:T(128)S(6)} %select_n.118), kind=kOutput, calls=%fused_computation.1.clone.1 | convolution fusion | flops 543160320 | bytes 9184260 | tf_op jit(solution)/shard_map/while/body/eval_jaxpr/igqd,pgd->igqp/dot_general | solution.py:66
  125.7 5.8 %fusion.84 = f32[128,128,16]{1,0,2:T(8,128)S(1)} fusion(f32[1024,128,16]{1,0,2:T(8,128)} %get-tuple-element.316, f32[128,16]{0,1:T(8,128)S(1)} %max.47, pred[1024]{0:T(1024)(128)(4,1)S(1)} %add_compare_fusion.3, bf16[8,1024,2,1,128]{4,1,3,2,0:T(8,128)(2,1)} %get-tuple-element.358, s32[]{:T(128)S(6)} %select_n.118), kind=kOutput, calls=%fused_computation.8.clone.1 | convolution fusion | flops 547356672 | bytes 9709572 | tf_op jit(solution)/shard_map/while/body/eval_jaxpr/igqp,pgd->igqd/dot_general | solution.py:87
  131.6 2.5 fusion.85
  134.2 1.4 bitcast_dynamic-update-slice_fusion.5
  139.5 5.5 %bitcast_reduce_fusion.2 = (f32[128,16]{0,1:T(8,128)S(1)}, f32[1024,128,16]{1,0,2:T(8,128)}) fusion(pred[1024]{0:T(1024)(128)(4,1)S(1)} %add_compare_fusion.3, bf16[128,1,16,128]{3,0,2,1:T(8,128)(2,1)S(1)} %get-tuple-element.361, bf16[8,1024,2,1,128]{4,1,3,2,0:T(8,128)(2,1)} %get-tuple-element.358, s32[]{:T(128)S(6)} %select_n.118), kind=kOutput, calls=%fused_computation.1.clone.1 | convolution fusion | flops 543160320 | bytes 9184260 | tf_op jit(solution)/shard_map/while/body/eval_jaxpr/igqd,pgd->igqp/dot_general | solution.py:66
  145.8 5.8 %fusion.84 = f32[128,128,16]{1,0,2:T(8,128)S(1)} fusion(f32[1024,128,16]{1,0,2:T(8,128)} %get-tuple-element.316, f32[128,16]{0,1:T(8,128)S(1)} %max.47, pred[1024]{0:T(1024)(128)(4,1)S(1)} %add_compare_fusion.3, bf16[8,1024,2,1,128]{4,1,3,2,0:T(8,128)(2,1)} %get-tuple-element.358, s32[]{:T(128)S(6)} %select_n.118), kind=kOutput, calls=%fused_computation.8.clone.1 | convolution fusion | flops 547356672 | bytes 9709572 | tf_op jit(solution)/shard_map/while/body/eval_jaxpr/igqp,pgd->igqd/dot_general | solution.py:87
  151.6 2.5 fusion.85
  154.3 1.3 bitcast_dynamic-update-slice_fusion.5
  159.6 5.5 %bitcast_reduce_fusion.2 = (f32[128,16]{0,1:T(8,128)S(1)}, f32[1024,128,16]{1,0,2:T(8,128)}) fusion(pred[1024]{0:T(1024)(128)(4,1)S(1)} %add_compare_fusion.3, bf16[128,1,16,128]{3,0,2,1:T(8,128)(2,1)S(1)} %get-tuple-element.361, bf16[8,1024,2,1,128]{4,1,3,2,0:T(8,128)(2,1)} %get-tuple-element.358, s32[]{:T(128)S(6)} %select_n.118), kind=kOutput, calls=%fused_computation.1.clone.1 | convolution fusion | flops 543160320 | bytes 9184260 | tf_op jit(solution)/shard_map/while/body/eval_jaxpr/igqd,pgd->igqp/dot_general | solution.py:66
  165.8 5.8 %fusion.84 = f32[128,128,16]{1,0,2:T(8,128)S(1)} fusion(f32[1024,128,16]{1,0,2:T(8,128)} %get-tuple-element.316, f32[128,16]{0,1:T(8,128)S(1)} %max.47, pred[1024]{0:T(1024)(128)(4,1)S(1)} %add_compare_fusion.3, bf16[8,1024,2,1,128]{4,1,3,2,0:T(8,128)(2,1)} %get-tuple-element.358, s32[]{:T(128)S(6)} %select_n.118), kind=kOutput, calls=%fused_computation.8.clone.1 | convolution fusion | flops 547356672 | bytes 9709572 | tf_op jit(solution)/shard_map/while/body/eval_jaxpr/igqp,pgd->igqd/dot_general | solution.py:87
  171.7 2.5 fusion.85
  174.3 1.3 bitcast_dynamic-update-slice_fusion.5
  179.6 5.5 %bitcast_reduce_fusion.2 = (f32[128,16]{0,1:T(8,128)S(1)}, f32[1024,128,16]{1,0,2:T(8,128)}) fusion(pred[1024]{0:T(1024)(128)(4,1)S(1)} %add_compare_fusion.3, bf16[128,1,16,128]{3,0,2,1:T(8,128)(2,1)S(1)} %get-tuple-element.361, bf16[8,1024,2,1,128]{4,1,3,2,0:T(8,128)(2,1)} %get-tuple-element.358, s32[]{:T(128)S(6)} %select_n.118), kind=kOutput, calls=%fused_computation.1.clone.1 | convolution fusion | flops 543160320 | bytes 9184260 | tf_op jit(solution)/shard_map/while/body/eval_jaxpr/igqd,pgd->igqp/dot_general | solution.py:66
  185.9 5.8 %fusion.84 = f32[128,128,16]{1,0,2:T(8,128)S(1)} fusion(f32[1024,128,16]{1,0,2:T(8,128)} %get-tuple-element.316, f32[128,16]{0,1:T(8,128)S(1)} %max.47, pred[1024]{0:T(1024)(128)(4,1)S(1)} %add_compare_fusion.3, bf16[8,1024,2,1,128]{4,1,3,2,0:T(8,128)(2,1)} %get-tuple-element.358, s32[]{:T(128)S(6)} %select_n.118), kind=kOutput, calls=%fused_computation.8.clone.1 | convolution fusion | flops 547356672 | bytes 9709572 | tf_op jit(solution)/shard_map/while/body/eval_jaxpr/igqp,pgd->igqd/dot_general | solution.py:87
  191.7 2.5 fusion.85
  199.6 5.5 %bitcast_reduce_fusion.2 = (f32[128,16]{0,1:T(8,128)S(1)}, f32[1024,128,16]{1,0,2:T(8,128)}) fusion(pred[1024]{0:T(1024)(128)(4,1)S(1)} %add_compare_fusion.3, bf16[128,1,16,128]{3,0,2,1:T(8,128)(2,1)S(1)} %get-tuple-element.361, bf16[8,1024,2,1,128]{4,1,3,2,0:T(8,128)(2,1)} %get-tuple-element.358, s32[]{:T(128)S(6)} %select_n.118), kind=kOutput, calls=%fused_computation.1.clone.1 | convolution fusion | flops 543160320 | bytes 9184260 | tf_op jit(solution)/shard_map/while/body/eval_jaxpr/igqd,pgd->igqp/dot_general | solution.py:66
  205.9 5.8 %fusion.84 = f32[128,128,16]{1,0,2:T(8,128)S(1)} fusion(f32[1024,128,16]{1,0,2:T(8,128)} %get-tuple-element.316, f32[128,16]{0,1:T(8,128)S(1)} %max.47, pred[1024]{0:T(1024)(128)(4,1)S(1)} %add_compare_fusion.3, bf16[8,1024,2,1,128]{4,1,3,2,0:T(8,128)(2,1)} %get-tuple-element.358, s32[]{:T(128)S(6)} %select_n.118), kind=kOutput, calls=%fused_computation.8.clone.1 | convolution fusion | flops 547356672 | bytes 9709572 | tf_op jit(solution)/shard_map/while/body/eval_jaxpr/igqp,pgd->igqd/dot_general | solution.py:87
  211.8 2.5 fusion.85
  214.4 1.4 bitcast_dynamic-update-slice_fusion.5
  219.7 5.5 %bitcast_reduce_fusion.2 = (f32[128,16]{0,1:T(8,128)S(1)}, f32[1024,128,16]{1,0,2:T(8,128)}) fusion(pred[1024]{0:T(1024)(128)(4,1)S(1)} %add_compare_fusion.3, bf16[128,1,16,128]{3,0,2,1:T(8,128)(2,1)S(1)} %get-tuple-element.361, bf16[8,1024,2,1,128]{4,1,3,2,0:T(8,128)(2,1)} %get-tuple-element.358, s32[]{:T(128)S(6)} %select_n.118), kind=kOutput, calls=%fused_computation.1.clone.1 | convolution fusion | flops 543160320 | bytes 9184260 | tf_op jit(solution)/shard_map/while/body/eval_jaxpr/igqd,pgd->igqp/dot_general | solution.py:66
  226.0 5.8 %fusion.84 = f32[128,128,16]{1,0,2:T(8,128)S(1)} fusion(f32[1024,128,16]{1,0,2:T(8,128)} %get-tuple-element.316, f32[128,16]{0,1:T(8,128)S(1)} %max.47, pred[1024]{0:T(1024)(128)(4,1)S(1)} %add_compare_fusion.3, bf16[8,1024,2,1,128]{4,1,3,2,0:T(8,128)(2,1)} %get-tuple-element.358, s32[]{:T(128)S(6)} %select_n.118), kind=kOutput, calls=%fused_computation.8.clone.1 | convolution fusion | flops 547356672 | bytes 9709572 | tf_op jit(solution)/shard_map/while/body/eval_jaxpr/igqp,pgd->igqd/dot_general | solution.py:87
  231.8 2.5 fusion.85
  234.5 1.4 bitcast_dynamic-update-slice_fusion.5
  239.8 5.5 %bitcast_reduce_fusion.2 = (f32[128,16]{0,1:T(8,128)S(1)}, f32[1024,128,16]{1,0,2:T(8,128)}) fusion(pred[1024]{0:T(1024)(128)(4,1)S(1)} %add_compare_fusion.3, bf16[128,1,16,128]{3,0,2,1:T(8,128)(2,1)S(1)} %get-tuple-element.361, bf16[8,1024,2,1,128]{4,1,3,2,0:T(8,128)(2,1)} %get-tuple-element.358, s32[]{:T(128)S(6)} %select_n.118), kind=kOutput, calls=%fused_computation.1.clone.1 | convolution fusion | flops 543160320 | bytes 9184260 | tf_op jit(solution)/shard_map/while/body/eval_jaxpr/igqd,pgd->igqp/dot_general | solution.py:66
  246.0 5.8 %fusion.84 = f32[128,128,16]{1,0,2:T(8,128)S(1)} fusion(f32[1024,128,16]{1,0,2:T(8,128)} %get-tuple-element.316, f32[128,16]{0,1:T(8,128)S(1)} %max.47, pred[1024]{0:T(1024)(128)(4,1)S(1)} %add_compare_fusion.3, bf16[8,1024,2,1,128]{4,1,3,2,0:T(8,128)(2,1)} %get-tuple-element.358, s32[]{:T(128)S(6)} %select_n.118), kind=kOutput, calls=%fused_computation.8.clone.1 | convolution fusion | flops 547356672 | bytes 9709572 | tf_op jit(solution)/shard_map/while/body/eval_jaxpr/igqp,pgd->igqd/dot_general | solution.py:87
  251.9 2.5 fusion.85
  256.0 4.8 %multiply_reduce_fusion = f32[128,16,128]{0,2,1:T(8,128)S(1)} fusion(f32[8,128,16,128]{1,3,2,0:T(8,128)} %get-tuple-element.146, f32[8,128,16]{1,2,0:T(8,128)S(1)} %get-tuple-element.236), kind=kLoop, calls=%fused_computation.46 | loop fusion | flops 3932160 | bytes 9502720 | tf_op jit(solution)/shard_map/reduce_sum | solution.py:111
  262.7 5.2 %all-to-all-start.2 = ((f32[4,32,2080]{2,1,0:T(8,128)}), f32[4,32,2080]{2,1,0:T(8,128)S(1)}, u32[]{:S(2)}, u32[]{:S(2)}) async-start(f32[4,32,2080]{2,1,0:T(8,128)} %concatenate.17), calls=%async_computation.2 | async-start | bytes 2228224 | tf_op jit(solution)/shard_map/all_to_all | solution.py:115
  269.1 13.1 %all-to-all-done.2 = f32[4,32,2080]{2,1,0:T(8,128)S(1)} async-done(((f32[4,32,2080]{2,1,0:T(8,128)}), f32[4,32,2080]{2,1,0:T(8,128)S(1)}, u32[]{:S(2)}, u32[]{:S(2)}) %all-to-all-start.2) | async-done | bytes 1064992 | tf_op jit(solution)/shard_map/all_to_all | solution.py:115
  (142 shorter events, 24.1 us)
Async XLA Ops:
  0.0 88.8 %copy-start = (bf16[32,128]{1,0:T(8,128)(2,1)S(1)}, bf16[32,128]{1,0:T(8,128)(2,1)}, u32[]{:S(2)}) copy-start(bf16[32,128]{1,0:T(8,128)(2,1)} %param.13) | copy-start | bytes 24580
  10.6 20.0 %all-to-all-start.1 = ((bf16[8,4,2048]{2,1,0:T(4,128)(2,1)}), bf16[8,4,2048]{2,1,0:T(4,128)(2,1)S(1)}, u32[]{:S(2)}, u32[]{:S(2)}) async-start(bf16[8,4,2048]{2,1,0:T(4,128)(2,1)} %constant_dynamic-update-slice_fusion), calls=%async_computation.1 | async-start | bytes 262144 | tf_op jit(solution)/shard_map/all_to_all | solution.py:42
  26.5 10.9 %copy-start.3 = (s32[8]{0:T(128)S(1)}, s32[8]{0:T(128)}, u32[]{:S(2)}) copy-start(s32[8]{0:T(128)} %param.17) | copy-start | bytes 100
  26.5 11.5 %copy-start.2 = (s32[8,128]{1,0:T(8,128)S(1)}, s32[8,128]{1,0:T(8,128)}, u32[]{:S(2)}) copy-start(s32[8,128]{1,0:T(8,128)} %param.15) | copy-start | bytes 12292
  30.7 58.3 %all-to-all-start = ((bf16[8,1024,256]{1,2,0:T(8,128)(2,1)}), bf16[8,1024,256]{1,2,0:T(8,128)(2,1)}, u32[]{:S(2)}, u32[]{:S(2)}) async-start(bf16[8,1024,256]{1,2,0:T(8,128)(2,1)} %pad_maximum_fusion), calls=%async_computation | async-start | bytes 8388608 | tf_op jit(solution)/shard_map/all_to_all | solution.py:48
  37.3 58.1 %copy-start.1 = (bf16[32,128]{1,0:T(8,128)(2,1)S(1)}, bf16[32,128]{1,0:T(8,128)(2,1)}, u32[]{:S(2)}) copy-start(bf16[32,128]{1,0:T(8,128)(2,1)} %param.14) | copy-start | bytes 24580
  105.6 5.9 %slice-start = ((s8[8388608]{0:T(1024)(128)(4,1)}), s8[4194304]{0:T(1024)(128)(4,1)S(1)}, s32[]{:S(2)}) async-start(s8[8388608]{0:T(1024)(128)(4,1)} %bitcast.176), calls=%async_computation.3 | async-start | bytes 8388608 | tf_op jit(solution)/shard_map/while
  105.7 5.9 %slice-start.1 = ((s8[8388608]{0:T(1024)(128)(4,1)}), s8[4194304]{0:T(1024)(128)(4,1)S(1)}, s32[]{:S(2)}) async-start(s8[8388608]{0:T(1024)(128)(4,1)} %bitcast.176), calls=%async_computation.4 | async-start | bytes 8388608 | tf_op jit(solution)/shard_map/while
  125.6 5.9 %slice-start = ((s8[8388608]{0:T(1024)(128)(4,1)}), s8[4194304]{0:T(1024)(128)(4,1)S(1)}, s32[]{:S(2)}) async-start(s8[8388608]{0:T(1024)(128)(4,1)} %bitcast.176), calls=%async_computation.3 | async-start | bytes 8388608 | tf_op jit(solution)/shard_map/while
  125.7 5.9 %slice-start.1 = ((s8[8388608]{0:T(1024)(128)(4,1)}), s8[4194304]{0:T(1024)(128)(4,1)S(1)}, s32[]{:S(2)}) async-start(s8[8388608]{0:T(1024)(128)(4,1)} %bitcast.176), calls=%async_computation.4 | async-start | bytes 8388608 | tf_op jit(solution)/shard_map/while
  145.7 5.9 %slice-start = ((s8[8388608]{0:T(1024)(128)(4,1)}), s8[4194304]{0:T(1024)(128)(4,1)S(1)}, s32[]{:S(2)}) async-start(s8[8388608]{0:T(1024)(128)(4,1)} %bitcast.176), calls=%async_computation.3 | async-start | bytes 8388608 | tf_op jit(solution)/shard_map/while
  145.8 5.9 %slice-start.1 = ((s8[8388608]{0:T(1024)(128)(4,1)}), s8[4194304]{0:T(1024)(128)(4,1)S(1)}, s32[]{:S(2)}) async-start(s8[8388608]{0:T(1024)(128)(4,1)} %bitcast.176), calls=%async_computation.4 | async-start | bytes 8388608 | tf_op jit(solution)/shard_map/while
  165.7 5.9 %slice-start = ((s8[8388608]{0:T(1024)(128)(4,1)}), s8[4194304]{0:T(1024)(128)(4,1)S(1)}, s32[]{:S(2)}) async-start(s8[8388608]{0:T(1024)(128)(4,1)} %bitcast.176), calls=%async_computation.3 | async-start | bytes 8388608 | tf_op jit(solution)/shard_map/while
  165.8 5.9 %slice-start.1 = ((s8[8388608]{0:T(1024)(128)(4,1)}), s8[4194304]{0:T(1024)(128)(4,1)S(1)}, s32[]{:S(2)}) async-start(s8[8388608]{0:T(1024)(128)(4,1)} %bitcast.176), calls=%async_computation.4 | async-start | bytes 8388608 | tf_op jit(solution)/shard_map/while
  185.8 5.9 %slice-start = ((s8[8388608]{0:T(1024)(128)(4,1)}), s8[4194304]{0:T(1024)(128)(4,1)S(1)}, s32[]{:S(2)}) async-start(s8[8388608]{0:T(1024)(128)(4,1)} %bitcast.176), calls=%async_computation.3 | async-start | bytes 8388608 | tf_op jit(solution)/shard_map/while
  185.9 5.9 %slice-start.1 = ((s8[8388608]{0:T(1024)(128)(4,1)}), s8[4194304]{0:T(1024)(128)(4,1)S(1)}, s32[]{:S(2)}) async-start(s8[8388608]{0:T(1024)(128)(4,1)} %bitcast.176), calls=%async_computation.4 | async-start | bytes 8388608 | tf_op jit(solution)/shard_map/while
  205.8 5.9 %slice-start = ((s8[8388608]{0:T(1024)(128)(4,1)}), s8[4194304]{0:T(1024)(128)(4,1)S(1)}, s32[]{:S(2)}) async-start(s8[8388608]{0:T(1024)(128)(4,1)} %bitcast.176), calls=%async_computation.3 | async-start | bytes 8388608 | tf_op jit(solution)/shard_map/while
  205.9 5.9 %slice-start.1 = ((s8[8388608]{0:T(1024)(128)(4,1)}), s8[4194304]{0:T(1024)(128)(4,1)S(1)}, s32[]{:S(2)}) async-start(s8[8388608]{0:T(1024)(128)(4,1)} %bitcast.176), calls=%async_computation.4 | async-start | bytes 8388608 | tf_op jit(solution)/shard_map/while
  225.9 5.9 %slice-start = ((s8[8388608]{0:T(1024)(128)(4,1)}), s8[4194304]{0:T(1024)(128)(4,1)S(1)}, s32[]{:S(2)}) async-start(s8[8388608]{0:T(1024)(128)(4,1)} %bitcast.176), calls=%async_computation.3 | async-start | bytes 8388608 | tf_op jit(solution)/shard_map/while
  226.0 5.9 %slice-start.1 = ((s8[8388608]{0:T(1024)(128)(4,1)}), s8[4194304]{0:T(1024)(128)(4,1)S(1)}, s32[]{:S(2)}) async-start(s8[8388608]{0:T(1024)(128)(4,1)} %bitcast.176), calls=%async_computation.4 | async-start | bytes 8388608 | tf_op jit(solution)/shard_map/while
  245.9 5.9 %slice-start = ((s8[8388608]{0:T(1024)(128)(4,1)}), s8[4194304]{0:T(1024)(128)(4,1)S(1)}, s32[]{:S(2)}) async-start(s8[8388608]{0:T(1024)(128)(4,1)} %bitcast.176), calls=%async_computation.3 | async-start | bytes 8388608 | tf_op jit(solution)/shard_map/while
  246.0 5.9 %slice-start.1 = ((s8[8388608]{0:T(1024)(128)(4,1)}), s8[4194304]{0:T(1024)(128)(4,1)S(1)}, s32[]{:S(2)}) async-start(s8[8388608]{0:T(1024)(128)(4,1)} %bitcast.176), calls=%async_computation.4 | async-start | bytes 8388608 | tf_op jit(solution)/shard_map/while
  256.0 11.9 %copy-start.4 = (s32[8]{0:T(128)S(1)}, s32[8]{0:T(128)}, u32[]{:S(2)}) copy-start(s32[8]{0:T(128)} %param.16) | copy-start | bytes 100
  262.7 19.5 %all-to-all-start.2 = ((f32[4,32,2080]{2,1,0:T(8,128)}), f32[4,32,2080]{2,1,0:T(8,128)S(1)}, u32[]{:S(2)}, u32[]{:S(2)}) async-start(f32[4,32,2080]{2,1,0:T(8,128)} %concatenate.17), calls=%async_computation.2 | async-start | bytes 2228224 | tf_op jit(solution)/shard_map/all_to_all | solution.py:115
